TPU v7x, 256 devices: a whole 4x4x8 slice. The times are simulated.
256 devices in a mesh: row: 16 (over y, z_lo, core), col: 16 (over x, z_hi).
Axes of the slice: x: 4, y: 4, z: 8 (z_hi: 4, z_lo: 2; z = z_hi * 2 + z_lo), core: 2. Of those that a mesh axis runs over, the one named last changes fastest.
Arguments:
- points: float32 [32, 24576], P(None, ('row', 'col')), may hold values from -6 to 6
- targets: float32 [24576], P(('row', 'col')), may hold values from -6 to 6
- probes: float32 [8, 24576], P(None, ('row', 'col')), may hold values from -6 to 6
- lengthscale: float32 [4], replicated, may hold values from 2.4 to 3.4
- outputscale: float32 [4], replicated, may hold values from 0.5 to 2
- noise_var: float32 [4], replicated, may hold values from 0.1 to 1
Outputs:
- solution: float32 [12, 24576], P(None, ('row', 'col'))
- residual: float32 [12, 24576], P(None, ('row', 'col'))
All inputs are finite; a program needn't handle non-finite values.
Results may differ from a plain program's by a relative error of at most 0.009.
Values may be sent and summed in bfloat16 or wider, within the bound.
A program may use at most 64 MiB of HBM per device.

v0:
```python
import math

import jax
import jax.numpy as jnp
from jax import lax
from jax.sharding import PartitionSpec as P

ITERATIONS = 2


def sq_distance(rows_x, cols_x):
    inner_prod = lax.dot_general(
        rows_x,
        cols_x,
        (((0,), (0,)), ((), ())),
        precision=lax.Precision.HIGHEST,
        preferred_element_type=jnp.float32,
    )
    sq_rows = jnp.sum(rows_x * rows_x, axis=0)
    sq_cols = jnp.sum(cols_x * cols_x, axis=0)
    return sq_rows[:, None] + sq_cols[None, :] - 2.0 * inner_prod


def make_tiles(distance, negscale, outputscale):
    return [
        (outputscale[p] * jnp.exp(distance * negscale[p])).astype(jnp.bfloat16)
        for p in range(negscale.shape[0])
    ]


def apply_tiles(tiles, dir_cols, width):
    products = []
    for p in range(len(tiles)):
        products.append(
            lax.dot_general(
                dir_cols[p * width : (p + 1) * width],
                tiles[p],
                (((1,), (1,)), ((), ())),
                preferred_element_type=jnp.float32,
            )
        )
    return jnp.concatenate(products, axis=0)


def on_device(points, targets, probes, lengthscale, outputscale, noise_var):
    n_part = lengthscale.shape[0]
    width = probes.shape[0] // n_part + 1
    right_side = jnp.concatenate(
        [
            jnp.concatenate(
                [targets[None, :], probes[p * (width - 1) : (p + 1) * (width - 1)]], axis=0
            )
            for p in range(n_part)
        ],
        axis=0,
    )
    negscale = -0.5 / (lengthscale * lengthscale)
    noisevec = jnp.repeat(noise_var, width)[:, None]
    rows_x = lax.all_gather(points, "col", axis=1, tiled=True)
    cols_x = lax.all_gather(points, "row", axis=1, tiled=True)
    row_count = rows_x.shape[1]
    row_block = math.gcd(row_count, 512)
    n_blocks = row_count // row_block
    kept = [
        make_tiles(
            sq_distance(rows_x[:, k * row_block : (k + 1) * row_block], cols_x),
            negscale,
            outputscale,
        )
        for k in range(n_blocks)
    ]
    solution = jnp.zeros_like(right_side)
    residual = right_side
    direction = right_side
    res_norm = lax.psum(jnp.sum(residual * residual, axis=1), ("row", "col"))
    for iteration in range(ITERATIONS):
        dir_cols = lax.all_gather(direction.astype(jnp.bfloat16), "row", axis=1, tiled=True)
        pieces = []
        for apply_k in range(n_blocks):
            tiles = kept[apply_k]
            pieces.append(apply_tiles(tiles, dir_cols, width))
        partial_value = jnp.concatenate(pieces, axis=1)
        applied = (
            lax.psum_scatter(partial_value, "col", scatter_dimension=1, tiled=True)
            + noisevec * direction
        )
        curvature = lax.psum(jnp.sum(direction * applied, axis=1), ("row", "col"))
        applied, curvature = (applied, curvature)
        step_size = (res_norm / curvature)[:, None]
        solution = solution + step_size * direction
        residual = residual - step_size * applied
        if iteration + 1 < ITERATIONS:
            fresh_norm = lax.psum(jnp.sum(residual * residual, axis=1), ("row", "col"))
            direction = residual + (fresh_norm / res_norm)[:, None] * direction
            res_norm = fresh_norm
    return (solution, residual)


def solution(mesh):
    placed = (P(None, ("row", "col")), P(("row", "col")), P(None, ("row", "col")), P(), P(), P())
    return jax.shard_map(
        on_device,
        mesh=mesh,
        in_specs=placed,
        out_specs=(P(None, ("row", "col")), P(None, ("row", "col"))),
        check_vma=False,
    )
```

profile of v0, /device:TPU:1, one launch (start us, length us, event | category | flops | bytes accessed | tf_op | source)
XLA Modules:
  0.0 570.3 jit_solution(6471585392873921023)
XLA Ops:
  7.2 22.9 %all-gather.2 = f32[16,96,32]{1,2,0:T(8,128)S(1)} all-gather(f32[1,96,32]{1,2,0:T(8,128)} %bitcast.68), channel_id=1, replica_groups=mesh['row'=16,'col'=16] {'row'}, dimensions={0}, use_global_device_ids=true | all-gather | bytes 208896 | tf_op jit(solution)/shard_map/all_gather | solution.py:60
  30.1 40.2 %all-gather.1 = f32[16,96,32]{1,2,0:T(8,128)S(1)} all-gather(f32[1,96,32]{1,2,0:T(8,128)} %bitcast.69), channel_id=1, replica_groups=mesh['row'=16,'col'=16] {'col'}, dimensions={0}, use_global_device_ids=true | all-gather | bytes 208896 | tf_op jit(solution)/shard_map/all_gather | solution.py:59
  72.7 23.2 %all-gather = bf16[16,96,12]{1,2,0:T(8,128)(2,1)S(1)} all-gather(bf16[1,96,12]{1,2,0:T(8,128)(2,1)S(1)} %convert_bitcast_fusion.1), channel_id=1, replica_groups=mesh['row'=16,'col'=16] {'row'}, dimensions={0}, use_global_device_ids=true | all-gather | bytes 39168 | tf_op jit(solution)/shard_map/all_gather | solution.py:77
  98.1 2.8 fusion
  101.0 3.7 fusion.1
  104.7 1.9 fusion.10
  106.6 1.9 fusion.18
  112.1 1.9 fusion.14
  114.0 1.9 fusion.6
  116.0 1.9 fusion.16
  117.8 1.9 fusion.8
  119.7 3.9 fusion.2
  123.6 1.8 fusion.20
  125.4 1.9 fusion.22
  127.4 1.9 fusion.24
  129.3 1.9 fusion.26
  132.7 77.2 %reduce-scatter.7.cloned.1.call-done = f32[96,12]{1,0:T(8,128)} async-done(((f32[1536,12]{1,0:T(8,128)}), f32[96,12]{1,0:T(8,128)}) %reduce-scatter.7.cloned.1.call-update) | async-done | bytes 4624
  210.9 75.8 %all-reduce = (f32[12]{0:T(128)S(1)}, f32[12]{0:T(128)S(1)}) all-reduce(f32[12]{0:T(128)S(1)} %get-tuple-element.6, f32[12]{0:T(128)S(1)} %get-tuple-element.5), channel_id=1, replica_groups=mesh['row'=16,'col'=16] {'row','col'}, use_global_device_ids=true, to_apply=%region_1.0 | all-reduce | flops 24 | bytes 192 | tf_op jit(solution)/shard_map/psum | solution.py:75
  286.9 73.4 %psum.30 = f32[12]{0:T(128)S(1)} all-reduce(f32[12]{0:T(128)S(1)} %multiply_reduce_fusion.5), channel_id=1, replica_groups=mesh['row'=16,'col'=16] {'row','col'}, use_global_device_ids=true, to_apply=%region_10.0 | all-reduce | flops 12 | bytes 96 | tf_op jit(solution)/shard_map/psum | solution.py:93
  360.4 19.8 %all-gather.3 = bf16[16,96,12]{1,2,0:T(8,128)(2,1)S(1)} all-gather(bf16[1,96,12]{1,2,0:T(8,128)(2,1)S(1)} %convert_bitcast_fusion), channel_id=1, replica_groups=mesh['row'=16,'col'=16] {'row'}, dimensions={0}, use_global_device_ids=true | all-gather | bytes 39168 | tf_op jit(solution)/shard_map/all_gather | solution.py:77
  380.4 4.0 fusion.3
  384.3 1.9 fusion.5
  386.3 1.9 fusion.7
  388.2 1.9 fusion.9
  391.9 1.9 fusion.13
  393.8 2.1 fusion.15
  396.0 1.9 fusion.17
  399.6 1.9 fusion.21
  401.6 1.9 fusion.23
  403.5 1.9 fusion.25
  406.6 79.3 %reduce-scatter.9.cloned.1.call-done = f32[96,12]{1,0:T(8,128)} async-done(((f32[1536,12]{1,0:T(8,128)}), f32[96,12]{1,0:T(8,128)}) %reduce-scatter.9.cloned.1.call-update) | async-done | bytes 4624
  487.0 75.8 %psum.31 = f32[12]{0:T(128)S(1)} all-reduce(f32[12]{0:T(128)S(1)} %multiply_reduce_fusion.4), channel_id=1, replica_groups=mesh['row'=16,'col'=16] {'row','col'}, use_global_device_ids=true, to_apply=%region_13.0 | all-reduce | flops 12 | bytes 96 | tf_op jit(solution)/shard_map/psum | solution.py:87
  (56 shorter events, 17.6 us)
Async XLA Ops:
  7.2 89.6 %copy-start.7 = (f32[4]{0:T(128)S(1)}, f32[4]{0:T(128)}, u32[]{:S(2)}) copy-start(f32[4]{0:T(128)} %param.9) | copy-start | bytes 52
  7.2 90.3 %copy-start.5 = (f32[4]{0:T(128)S(1)}, f32[4]{0:T(128)}, u32[]{:S(2)}) copy-start(f32[4]{0:T(128)} %param.10) | copy-start | bytes 52
  7.2 202.6 %reduce-scatter.7.cloned.1.call-start = ((), (), s32[]{:S(2)}) async-start(), calls=%async_computation.2 | async-start | bytes 835584
  96.7 4.3 copy-start.4
  101.0 16.9 %copy-start.2 = (f32[512,1536]{1,0:T(8,128)}, f32[512,1536]{1,0:T(8,128)S(1)}, u32[]{:S(2)}) copy-start(f32[512,1536]{1,0:T(8,128)S(1)} %fusion) | copy-start | bytes 9437188
  123.6 5.7 copy-start
  129.2 3.2 copy-start.6
  132.4 353.5 %reduce-scatter.9.cloned.1.call-start = ((), (), s32[]{:S(2)}) async-start(), calls=%async_computation.3 | async-start | bytes 835584
  380.4 4.0 copy-start.3
  393.8 4.1 copy-start.1
Sparse Core Ops, SparseCore 0:
  132.6 77.2 reduce-scatter.6
  406.8 79.0 reduce-scatter.8
where the time goes:
time: 571 us; the launch traced here: 570 us
  blocking collectives  331 us (58%)
  waiting for transfers between devices  156 us (27%)
  matrix products  58 us (10%)
  between operations  14.2 us (2%)
  local copies, waits for them, and re-layouts  8.85 us (2%)
    unnamed x4, waiting for transfers between devices  156 us
    psum x1, blocking collectives, on_device(): res_norm = lax.psum(jnp.sum(residual * residual, axis=1), ('row', 'col'))  75.8 us
    psum x1, blocking collectives, on_device(): curvature = lax.psum(jnp.sum(direction * applied, axis=1), ('row', 'col'))  75.8 us
    psum x1, blocking collectives, on_device(): fresh_norm = lax.psum(jnp.sum(residual * residual, axis=1), ('row', 'col'))  73.4 us
    dot_general x24, matrix products, apply_tiles(): lax.dot_general(dir_cols[p * width:(p + 1) * width], tiles[p], (((1,), (1...  47.6 us
    all_gather x2, blocking collectives, on_device(): lax.all_gather(direction.astype(jnp.bfloat16), 'row', axis=1, tiled=True)  43 us
    all_gather x1, blocking collectives, on_device(): rows_x = lax.all_gather(points, 'col', axis=1, tiled=True)  40.2 us
    all_gather x1, blocking collectives, on_device(): cols_x = lax.all_gather(points, 'row', axis=1, tiled=True)  22.9 us
  transfers between devices with their start and end apart: 2, of which 2 were waited for; matrix products, arithmetic and copies ran while one was open for 0% of the time, Pallas kernels for 0%

commit v1 on v0

v1 whole, which is shorter than its diff:
```python
import functools
import math

import jax
import jax.numpy as jnp
from jax import lax
from jax.experimental import pallas as pl
from jax.experimental.pallas import tpu as pltpu
from jax.sharding import PartitionSpec as P

ITERATIONS = 2
ROWS = 16
LANES = 128
TILE = 256
LOG2E = math.log2(math.e)
F32 = jnp.float32
BF16 = jnp.bfloat16
MESH = pl.DeviceIdType.MESH


def split3(x):
    hi = x.astype(BF16).astype(F32)
    rest = x - hi
    mid = rest.astype(BF16).astype(F32)
    low = (rest - mid).astype(BF16).astype(F32)
    return hi, mid, low


def norm_rows(parts, ones_first):
    at = lax.broadcasted_iota(jnp.int32, (16, parts[0].shape[1]), 0)
    start = 3 if ones_first else 0
    out = jnp.where((at < 3) if ones_first else ((at >= 3) & (at < 6)), 1.0, 0.0).astype(F32)
    for k in range(3):
        out = jnp.where(at == start + k, parts[k], out)
    return out


def compact(dst, slots, first, rows, count, width):
    for k in range(count):
        dst[:, k * width : (k + 1) * width] = slots[k, first : first + rows, :width]


def kernel(
    n_red,
    n_con,
    width,
    per,
    points,
    targets,
    probes,
    lengthscale,
    outputscale,
    noise_var,
    sol_out,
    res_out,
    msg,
    con_in,
    red_in,
    con_lhs,
    red_x,
    red_rhs,
    con_d,
    red_d,
    con_a,
    red_a,
    blocks,
    kept,
    product,
    rs_send,
    rs_recv,
    ag_send,
    ag_con,
    ag_red,
    nrm_send,
    nrm_recv,
    rs2_send,
    rs2_recv,
    fin_send,
    fin_recv,
    send_sem,
    recv_sem,
):
    n_part = lengthscale.shape[0]
    feats = points.shape[0]
    count = n_part * per
    span = n_con * width
    wide = n_red * width
    me_red = lax.axis_index("row")
    me_con = lax.axis_index("col")

    def red_peer(step):
        at = lax.rem(me_red + step, n_red)
        return at, (at, me_con)

    def con_peer(step):
        at = lax.rem(me_con + step, n_con)
        return at, (me_red, at)

    barrier = pltpu.get_barrier_semaphore()
    for step in range(1, n_red):
        pl.semaphore_signal(barrier, inc=1, device_id=red_peer(step)[1], device_id_type=MESH)
    for step in range(1, n_con):
        pl.semaphore_signal(barrier, inc=1, device_id=con_peer(step)[1], device_id_type=MESH)

    msg[...] = jnp.zeros_like(msg)
    msg[0:feats, 0:width] = points[...]
    for p in range(n_part):
        at = feats + p * per
        msg[at : at + 1, 0:width] = targets[...]
        msg[at + 1 : at + per, 0:width] = probes[p * (per - 1) : (p + 1) * (per - 1), :]

    row_at = lax.broadcasted_iota(jnp.int32, (ROWS, 1), 0)
    lane_at = lax.broadcasted_iota(jnp.int32, (ROWS, LANES), 1)
    live = row_at < count
    noise = jnp.zeros((ROWS, 1), F32)
    for p in range(n_part):
        noise = jnp.where((row_at >= p * per) & (row_at < (p + 1) * per), noise_var[p], noise)

    pl.semaphore_wait(barrier, n_red - 1 + n_con - 1)

    def send(phase, peer, src, dst):
        pltpu.make_async_remote_copy(
            src_ref=src,
            dst_ref=dst,
            send_sem=send_sem.at[phase],
            recv_sem=recv_sem.at[phase],
            device_id=peer,
            device_id_type=MESH,
        ).start()

    def to_con(phase, src, slots):
        for step in range(1, n_con):
            send(phase, con_peer(step)[1], src, slots.at[me_con])

    def to_red(phase, src, slots):
        for step in range(1, n_red):
            send(phase, red_peer(step)[1], src, slots.at[me_red])

    def arrive(sem, slots, n):
        some = slots.at[pl.ds(0, n - 1)]
        pltpu.make_async_copy(some, some, sem).wait()

    to_con(0, msg, con_in)
    to_red(1, msg, red_in)
    con_in[me_con] = msg[...]
    red_in[me_red] = msg[...]
    arrive(recv_sem.at[0], con_in, n_con)

    pad = jnp.zeros((TILE - 6 * feats - 16, LANES), F32)

    def con_block(k, _):
        x = con_in[k, 0:feats, :]
        hi, mid, low = split3(x)
        norms = norm_rows(split3(jnp.sum(x * x, axis=0, keepdims=True)), False)
        full = jnp.concatenate([hi, hi, mid, hi, mid, low, norms, pad], axis=0)
        con_lhs[pl.ds(pl.multiple_of(k * width, 32), width), :] = jnp.transpose(full)[0:width].astype(BF16)
        return 0

    lax.fori_loop(0, n_con, con_block, 0)
    compact(con_d, con_in, feats, ROWS, n_con, width)

    def spread(direction):
        for p in range(n_part):
            mine = (row_at >= p * per) & (row_at < (p + 1) * per)
            blocks[:, p * span : (p + 1) * span] = jnp.where(mine, direction, 0.0).astype(BF16)

    spread(con_d[...])

    arrive(recv_sem.at[1], red_in, n_red)
    compact(red_x, red_in, 0, feats, n_red, width)
    compact(red_d, red_in, feats, ROWS, n_red, width)
    x = red_x[...]
    hi, mid, low = split3(x)
    norms = norm_rows(split3(jnp.sum(x * x, axis=0, keepdims=True)), True)
    hi, mid, low = (-2.0 * hi, -2.0 * mid, -2.0 * low)
    pad2 = jnp.zeros((TILE - 6 * feats - 16, wide), F32)
    red_rhs[...] = jnp.concatenate([hi, mid, hi, low, mid, hi, norms, pad2], axis=0).astype(BF16)

    scales = []
    for p in range(n_part):
        length = jnp.full((1, TILE), lengthscale[p], F32)
        scales.append(((-0.5 * LOG2E) / (length * length), jnp.full((1, TILE), outputscale[p], F32)))

    product[...] = jnp.zeros_like(product)

    def build(ib, _):
        at = pl.multiple_of(ib * TILE, TILE)
        lhs = con_lhs[pl.ds(at, TILE), :]
        for jb in range(wide // TILE):
            cols = slice(jb * TILE, (jb + 1) * TILE)
            distance = jnp.dot(lhs, red_rhs[:, cols], preferred_element_type=F32)
            total = product[:, cols]
            for p in range(n_part):
                kern = (scales[p][1] * jnp.exp2(distance * scales[p][0])).astype(BF16)
                here = pl.ds(pl.multiple_of(p * span + at, TILE), TILE)
                kept[here, cols] = kern
                total = total + jnp.dot(blocks[:, here], kern, preferred_element_type=F32)
            product[:, cols] = total
        return 0

    lax.fori_loop(0, span // TILE, build, 0)

    def scatter(phase, buf, slots, extra):
        for k in range(n_red):
            part = product[:, k * width : (k + 1) * width]
            buf[k, :, 0:width] = part
            buf[k, :, width:LANES] = jnp.broadcast_to(extra, (ROWS, LANES - width))
        for step in range(1, n_red):
            at, peer = red_peer(step)
            send(phase, peer, buf.at[at], slots.at[me_red])
        slots[me_red] = buf[me_red]
        arrive(recv_sem.at[phase], slots, n_red)
        return jnp.sum(slots[...], axis=0)

    mid_lane = (width + LANES) // 2
    own_d = msg[feats : feats + ROWS, :]
    d_con = con_d[...]
    d_red = red_d[...]
    a_own = scatter(2, rs_send, rs_recv, jnp.sum(d_red * product[...], axis=1, keepdims=True))
    a_own = a_own + jnp.where(lane_at < width, noise * own_d, 0.0)
    norm_red = jnp.sum(d_red * d_red, axis=1, keepdims=True)
    ag_send[...] = jnp.where(lane_at < mid_lane, a_own, norm_red)
    to_con(3, ag_send, ag_con)
    to_red(4, ag_send, ag_red)
    ag_con[me_con] = ag_send[...]
    ag_red[me_red] = ag_send[...]

    def totals(slots):
        total = jnp.sum(slots[...], axis=0)
        return total[:, width : width + 1], total[:, mid_lane : mid_lane + 1]

    arrive(recv_sem.at[3], ag_con, n_con)
    curve_kern, res_norm = totals(ag_con)
    curvature = curve_kern + noise * res_norm
    step_size = res_norm / jnp.where(live, curvature, 1.0)
    compact(con_a, ag_con, 0, ROWS, n_con, width)
    r_con = d_con - step_size * con_a[...]
    nrm_send[...] = jnp.broadcast_to(jnp.sum(r_con * r_con, axis=1, keepdims=True), (ROWS, LANES))
    to_red(5, nrm_send, nrm_recv)
    nrm_recv[me_red] = nrm_send[...]
    arrive(recv_sem.at[4], ag_red, n_red)
    compact(red_a, ag_red, 0, ROWS, n_red, width)
    r_red = d_red - step_size * red_a[...]
    arrive(recv_sem.at[5], nrm_recv, n_red)
    fresh_norm = jnp.sum(nrm_recv[...], axis=0)[:, 0:1]
    beta = fresh_norm / jnp.where(live, res_norm, 1.0)
    spread(r_con + beta * d_con)
    d1_red = r_red + beta * d_red
    r_own = own_d - step_size * a_own
    d1_own = r_own + beta * own_d

    for jb in range(wide // TILE):
        cols = slice(jb * TILE, (jb + 1) * TILE)
        product[:, cols] = jnp.dot(blocks[...], kept[:, cols], preferred_element_type=F32)

    a1_own = scatter(6, rs2_send, rs2_recv, jnp.sum(d1_red * product[...], axis=1, keepdims=True))
    norm1_red = jnp.sum(d1_red * d1_red, axis=1, keepdims=True)
    fin_send[...] = jnp.where(lane_at < mid_lane, a1_own, norm1_red)
    to_con(7, fin_send, fin_recv)
    fin_recv[me_con] = fin_send[...]
    a1_own = a1_own + noise * d1_own
    arrive(recv_sem.at[7], fin_recv, n_con)
    curve_kern1, d1_norm = totals(fin_recv)
    curvature1 = curve_kern1 + noise * d1_norm
    step1 = fresh_norm / jnp.where(live, curvature1, 1.0)
    sol = step_size * own_d + step1 * d1_own
    res = r_own - step1 * a1_own
    sol_out[...] = sol[0:count, 0:width]
    res_out[...] = res[0:count, 0:width]

    for phase, slots, n in (
        (0, con_in, n_con),
        (1, red_in, n_red),
        (2, rs_recv, n_red),
        (3, ag_con, n_con),
        (4, ag_red, n_red),
        (5, nrm_recv, n_red),
        (6, rs2_recv, n_red),
        (7, fin_recv, n_con),
    ):
        arrive(send_sem.at[phase], slots, n)


def solution(mesh):
    n_red, n_con = mesh.shape["row"], mesh.shape["col"]

    def on_device(points, targets, probes, lengthscale, outputscale, noise_var):
        feats, width = points.shape
        n_part = lengthscale.shape[0]
        per = probes.shape[0] // n_part + 1
        count = n_part * per
        span, wide = n_con * width, n_red * width
        vmem = pl.BlockSpec(memory_space=pltpu.VMEM)
        smem = pl.BlockSpec(memory_space=pltpu.SMEM)
        out = jax.ShapeDtypeStruct((count, width), F32)

        def slots(n):
            return pltpu.VMEM((n, ROWS, LANES), F32)

        return pl.pallas_call(
            functools.partial(kernel, n_red, n_con, width, per),
            out_shape=(out, out),
            in_specs=[vmem] * 3 + [smem] * 3,
            out_specs=(vmem, vmem),
            scratch_shapes=[
                pltpu.VMEM((feats + ROWS, LANES), F32),
                pltpu.VMEM((n_con, feats + ROWS, LANES), F32),
                pltpu.VMEM((n_red, feats + ROWS, LANES), F32),
                pltpu.VMEM((span, TILE), BF16),
                pltpu.VMEM((feats, wide), F32),
                pltpu.VMEM((TILE, wide), BF16),
                pltpu.VMEM((ROWS, span), F32),
                pltpu.VMEM((ROWS, wide), F32),
                pltpu.VMEM((ROWS, span), F32),
                pltpu.VMEM((ROWS, wide), F32),
                pltpu.VMEM((ROWS, n_part * span), BF16),
                pltpu.VMEM((n_part * span, wide), BF16),
                pltpu.VMEM((ROWS, wide), F32),
                slots(n_red),
                slots(n_red),
                pltpu.VMEM((ROWS, LANES), F32),
                slots(n_con),
                slots(n_red),
                pltpu.VMEM((ROWS, LANES), F32),
                slots(n_red),
                slots(n_red),
                slots(n_red),
                pltpu.VMEM((ROWS, LANES), F32),
                slots(n_con),
                pltpu.SemaphoreType.DMA((8,)),
                pltpu.SemaphoreType.DMA((8,)),
            ],
            compiler_params=pltpu.CompilerParams(
                collective_id=0, has_side_effects=True, vmem_limit_bytes=56 * 2**20
            ),
            name="cg_solve",
        )(points, targets[None, :], probes, lengthscale, outputscale, noise_var)

    both = P(None, ("row", "col"))
    return jax.shard_map(
        on_device,
        mesh=mesh,
        in_specs=(both, P(("row", "col")), both, P(), P(), P()),
        out_specs=(both, both),
        check_vma=False,
    )
```

time: 571 us -> 73.1 us (0.13)
  blocking collectives: 331 us -> 0 us
  waiting for transfers between devices: 156 us -> 0 us
  Pallas kernels: 0 us -> 70.1 us
  matrix products: 58 us -> 0 us
  between operations: 14.2 us -> 0.65 us
  local copies, waits for them, and re-layouts: 8.85 us -> 1.9 us
    psum x3 -> x0, blocking collectives: 225 us -> none  [the longest x1 75.8 us: on_device(): res_norm = lax.psum(jnp.sum(residual * residual, axis=1), ('row', 'col'))]
    unnamed x4 -> x0, waiting for transfers between devices: 156 us -> none
    all_gather x4 -> x0, blocking collectives: 106 us -> none  [the longest x2 43 us: on_device(): lax.all_gather(direction.astype(jnp.bfloat16), 'row', axis=1, tiled=True)]
    pallas_call x0 -> x1, Pallas kernels: none -> 70.1 us  [on_device(): pl.pallas_call(functools.partial(kernel, n_red, n_con, width, per), out_s...]
    dot_general x27 -> x0, matrix products: 58 us -> none  [the longest x24 47.6 us: apply_tiles(): lax.dot_general(dir_cols[p * width:(p + 1) * width], tiles[p], (((1,), (1...]
  transfers between devices with their start and end apart: 2 -> 0, of which waited for: 2 -> 0; matrix products, arithmetic and copies ran while one was open for 0% -> 0% of each run, Pallas kernels for 0% -> 0%
where the time goes in v1:
time: 73.1 us; the launch traced here: 72.7 us
  Pallas kernels  70.1 us (96%)
  local copies, waits for them, and re-layouts  1.9 us (3%)
    pallas_call x1, Pallas kernels, on_device(): pl.pallas_call(functools.partial(kernel, n_red, n_con, width, per), out_s...  70.1 us
    unnamed x4, local copies, waits for them, and re-layouts  1.9 us

profile of v1, /device:TPU:1, one launch (start us, length us, event | category | flops | bytes accessed | tf_op | source)
XLA Modules:
  0.0 72.7 jit_solution(16884203851837425680)
XLA Ops:
  0.6 70.1 %cg_solve.1 = (f32[12,96]{1,0:T(8,128)}, f32[12,96]{1,0:T(8,128)}) custom-call(f32[32,96]{1,0:T(8,128)} %points.1, f32[1,96]{1,0:T(1,128)} %bitcast.1, f32[8,96]{1,0:T(8,128)} %probes.1, f32[4]{0:T(128)} %lengthscale.1, f32[4]{0:T(128)} %outputscale.1, f32[4]{0:T(128)} %noise_var.1), custom_call_target="tpu_custom_call" | custom-call | tf_op jit(solution)/shard_map/cg_solve/pallas_call | solution.py:300
  70.8 0.0 copy-start
  70.8 1.3 %copy.10 = f32[12,96]{1,0:T(8,128)} copy(f32[12,96]{1,0:T(8,128)} %get-tuple-element.4) | data formatting | bytes 9216
  72.1 0.0 copy-done
  72.1 0.6 copy.11
Async XLA Ops:
  70.8 1.3 %copy-start = (f32[12,96]{1,0:T(8,128)S(1)}, f32[12,96]{1,0:T(8,128)}, u32[]{:S(2)}) copy-start(f32[12,96]{1,0:T(8,128)} %get-tuple-element.5) | copy-start | bytes 13828

commit v2 on v1

v2 whole, which is shorter than its diff:
```python
import functools
import math

import jax
import jax.numpy as jnp
from jax import lax
from jax.experimental import pallas as pl
from jax.experimental.pallas import tpu as pltpu
from jax.sharding import PartitionSpec as P

LANES = 128
TILE = 256
CHUNK = 32
LOG2E = math.log2(math.e)
F32 = jnp.float32
BF16 = jnp.bfloat16
MESH = pl.DeviceIdType.MESH
NX, NY, NZ, CORES = 4, 4, 8, 2


def split3(x):
    hi = x.astype(BF16).astype(F32)
    rest = x - hi
    mid = rest.astype(BF16).astype(F32)
    low = (rest - mid).astype(BF16).astype(F32)
    return hi, mid, low


def norm_rows(parts, ones_first):
    at = lax.broadcasted_iota(jnp.int32, (16, parts[0].shape[1]), 0)
    start = 3 if ones_first else 0
    out = jnp.where((at < 3) if ones_first else ((at >= 3) & (at < 6)), 1.0, 0.0).astype(F32)
    for k in range(3):
        out = jnp.where(at == start + k, parts[k], out)
    return out


def kernel(
    width,
    per,
    points_hbm,
    targets_hbm,
    probes_hbm,
    lengthscale_hbm,
    outputscale_hbm,
    noise_hbm,
    sol_out,
    res_out,
    points,
    targets,
    probes,
    lengthscale,
    outputscale,
    noise_var,
    rhs,
    msg,
    con_in,
    red_in,
    red_rhs_in,
    con_lhs,
    con_dt,
    red_x,
    red_op,
    con_d,
    red_d,
    con_a,
    red_a,
    blocks,
    dist,
    kept,
    product,
    rs_send,
    rs_recv,
    ag_send,
    ag_con,
    ag_red,
    nrm_send,
    nrm_recv,
    rs2_send,
    rs2_recv,
    crv_send,
    crv_recv,
    fin_send,
    fin_recv,
    load_sem,
    send_sem,
    recv_sem,
    con_sem,
):
    n_red, n_con = NX * NY, NZ * CORES
    n_part = lengthscale.shape[0]
    feats = points.shape[0]
    groups = feats // 8
    count = n_part * per
    pair = CORES * width
    span = n_con * width
    wide = n_red * width
    base = feats * width // 8

    loads = [
        pltpu.make_async_copy(a, b, load_sem.at[k])
        for k, (a, b) in enumerate(
            (
                (points_hbm, points),
                (targets_hbm, targets),
                (probes_hbm, probes),
                (lengthscale_hbm, lengthscale),
                (outputscale_hbm, outputscale),
                (noise_hbm, noise_var),
            )
        )
    ]
    for load in loads:
        load.start()

    at_row, at_col = lax.axis_index("row"), lax.axis_index("col")
    at_y, z_lo, core = at_row // 4, lax.rem(at_row // 2, 2), lax.rem(at_row, 2)
    at_x, z_hi = at_col // 4, lax.rem(at_col, 4)
    at_z = z_hi * 2 + z_lo
    me_red, me_con = at_x * NY + at_y, at_z * CORES + core

    def red_peer(step):
        at = lax.rem(me_red + step, n_red)
        return at, (lax.rem(at, NY) * 4 + z_lo * 2 + core, (at // NY) * 4 + z_hi)

    def near_z(t):
        away = ((t + 1) // 2) * (2 * lax.rem(t, 2) - 1)
        return lax.rem(at_z + away + NZ, NZ)

    def con_peer(z, c):
        return z * CORES + c, (at_y * 4 + lax.rem(z, 2) * 2 + c, at_x * 4 + z // 2)

    near = [near_z(t) for t in range(NZ)]
    con_peers = [con_peer(at_z, 1 - core)]
    for t in range(1, NZ):
        con_peers += [con_peer(near[t], core), con_peer(near[t], 1 - core)]
    red_peers = [red_peer(step) for step in range(1, n_red)]

    def arrive(sem, slots, n):
        some = slots.at[pl.ds(0, n - 1)]
        pltpu.make_async_copy(some, some, sem).wait()

    def drain(phases):
        buffers = (con_in, red_in, rs_recv, ag_con, ag_red, nrm_recv, rs2_recv, fin_recv, crv_recv, red_rhs_in)
        for phase in phases:
            arrive(send_sem.at[phase], buffers[phase], buffers[phase].shape[0])

    barrier = pltpu.get_barrier_semaphore()
    for _, peer in con_peers + red_peers:
        pl.semaphore_signal(barrier, inc=1, device_id=peer, device_id_type=MESH)

    msg[...] = jnp.zeros_like(msg)
    rhs[...] = jnp.zeros_like(rhs)
    for load in loads:
        load.wait()
    for q in range(groups):
        msg[:, q * width : (q + 1) * width] = points[8 * q : 8 * q + 8, :]
    for p in range(n_part):
        rhs[p * per : p * per + 1, 0:width] = targets[...]
        rhs[p * per + 1 : (p + 1) * per, 0:width] = probes[p * (per - 1) : (p + 1) * (per - 1), :]
    msg[:, base : base + width] = rhs[0:8, 0:width]
    msg[0 : count - 8, base + width : base + 2 * width] = rhs[8:count, 0:width]

    row_at = lax.broadcasted_iota(jnp.int32, (count, 1), 0)
    lane_at = lax.broadcasted_iota(jnp.int32, (count, LANES), 1)
    mine = [(row_at >= p * per) & (row_at < (p + 1) * per) for p in range(n_part)]
    noise = jnp.zeros((count, 1), F32)
    for p in range(n_part):
        noise = jnp.where(mine[p], noise_var[p], noise)
    scales = []
    for p in range(n_part):
        length = jnp.full((1, TILE), lengthscale[p], F32)
        scales.append(((-0.5 * LOG2E) / (length * length), jnp.full((1, TILE), outputscale[p], F32)))
    product[...] = jnp.zeros_like(product)

    pl.semaphore_wait(barrier, n_red - 1 + n_con - 1)

    def send(phase, peer, src, dst, sem=None):
        pltpu.make_async_remote_copy(
            src_ref=src,
            dst_ref=dst,
            send_sem=send_sem.at[phase],
            recv_sem=recv_sem.at[phase] if sem is None else sem,
            device_id=peer,
            device_id_type=MESH,
        ).start()

    def to_con(phase, src, slots):
        for _, peer in con_peers:
            send(phase, peer, src, slots.at[me_con])

    def to_red(phase, src, slots):
        for _, peer in red_peers:
            send(phase, peer, src, slots.at[me_red])

    for _, peer in con_peers[:5]:
        send(0, peer, msg, con_in.at[me_con], con_sem.at[me_con])
    to_red(1, msg.at[:, 0:base], red_in)
    for _, peer in con_peers[5:]:
        send(0, peer, msg, con_in.at[me_con], con_sem.at[me_con])
    to_red(9, msg.at[:, base:], red_rhs_in)
    con_in[me_con] = msg[...]
    red_in[me_red] = msg[:, 0:base]
    red_rhs_in[me_red] = msg[:, base:]

    pad = jnp.zeros((TILE - 6 * feats - 16, LANES), F32)

    def con_wait(slot):
        pltpu.make_async_copy(con_in.at[slot], con_in.at[slot], con_sem.at[slot]).wait()

    def prepare(t, z, buf):
        for c in range(CORES):
            slot = z * CORES + c
            x = jnp.concatenate(
                [con_in[slot, :, q * width : q * width + LANES] for q in range(groups)], axis=0
            )
            hi, mid, low = split3(x)
            norms = norm_rows(split3(jnp.sum(x * x, axis=0, keepdims=True)), False)
            full = jnp.concatenate([hi, hi, mid, hi, mid, low, norms, pad], axis=0)
            con_lhs[buf, c * width : (c + 1) * width, :] = jnp.transpose(full)[0:width].astype(BF16)
            con_dt[t, 0:8, c * width : (c + 1) * width] = con_in[slot, :, base : base + width]
            con_dt[t, 8:count, c * width : (c + 1) * width] = con_in[
                slot, 0 : count - 8, base + width : base + 2 * width
            ]

    def build(t, buf):
        low = con_dt[t, :, 0:pair]
        sides = [jnp.where(mine[p], low, 0.0).astype(BF16) for p in range(n_part)]
        lhs = con_lhs[buf]
        for jb in range(wide // TILE):
            cols = slice(jb * TILE, (jb + 1) * TILE)
            dist[jb] = jnp.dot(lhs, red_op[:, cols], preferred_element_type=F32)
        for jb in range(wide // TILE):
            cols = slice(jb * TILE, (jb + 1) * TILE)
            for r in range(pair // CHUNK):
                part = dist[jb, r * CHUNK : (r + 1) * CHUNK, :]
                for p in range(n_part):
                    kern = (scales[p][1] * jnp.exp2(part * scales[p][0])).astype(BF16)
                    at = pl.multiple_of(p * span + t * pair + r * CHUNK, CHUNK)
                    kept[pl.ds(at, CHUNK), cols] = kern
            total = product[:, cols]
            for p in range(n_part):
                at = pl.multiple_of(p * span + t * pair, CHUNK)
                total = total + jnp.dot(sides[p], kept[pl.ds(at, pair), cols], preferred_element_type=F32)
            product[:, cols] = total

    con_wait(at_z * CORES + 1 - core)
    prepare(0, at_z, 0)

    arrive(recv_sem.at[1], red_in, n_red)
    for k in range(n_red):
        for q in range(groups):
            red_x[8 * q : 8 * q + 8, k * width : (k + 1) * width] = red_in[k, :, q * width : (q + 1) * width]
    x = red_x[...]
    hi, mid, low = split3(x)
    norms = norm_rows(split3(jnp.sum(x * x, axis=0, keepdims=True)), True)
    hi, mid, low = (-2.0 * hi, -2.0 * mid, -2.0 * low)
    pad2 = jnp.zeros((TILE - 6 * feats - 16, wide), F32)
    red_op[...] = jnp.concatenate([hi, mid, hi, low, mid, hi, norms, pad2], axis=0).astype(BF16)

    def step(t, _):
        z = near_z(t + 1)
        con_wait(z * CORES)
        con_wait(z * CORES + 1)
        build(t, lax.rem(t, 2))
        prepare(t + 1, z, lax.rem(t + 1, 2))
        return 0

    lax.fori_loop(0, NZ - 1, step, 0)
    build(NZ - 1, (NZ - 1) % 2)

    arrive(recv_sem.at[9], red_rhs_in, n_red)
    for k in range(n_red):
        red_d[0:8, k * width : (k + 1) * width] = red_rhs_in[k, :, 0:width]
        red_d[8:count, k * width : (k + 1) * width] = red_rhs_in[k, 0 : count - 8, width : 2 * width]

    def chunk_out(k, buf, extra):
        buf[k, :, 0:width] = product[:, k * width : (k + 1) * width]
        buf[k, :, width:LANES] = jnp.broadcast_to(extra, (count, LANES - width))

    def to_row(column, offset):
        return jnp.sum(jnp.where(lane_at == row_at + offset, column, 0.0), axis=0, keepdims=True)

    def to_column(row, offset):
        return jnp.sum(jnp.where(lane_at == row_at + offset, row, 0.0), axis=1, keepdims=True)

    mid_lane = (width + LANES) // 2
    own_d = rhs[...]
    d_red = red_d[...]
    partial_curve = jnp.sum(d_red * product[...], axis=1, keepdims=True)
    for k in range(n_red):
        chunk_out(k, rs_send, partial_curve)
    for at, peer in red_peers:
        send(2, peer, rs_send.at[at], rs_recv.at[me_red])
    rs_recv[me_red] = rs_send[me_red]
    for t in range(NZ):
        con_d[:, t * pair : (t + 1) * pair] = con_dt[t, :, 0:pair]
    d_con = con_d[...]
    norm_red = jnp.sum(d_red * d_red, axis=1, keepdims=True)
    arrive(recv_sem.at[2], rs_recv, n_red)
    a_own = jnp.sum(rs_recv[...], axis=0)
    a_own = a_own + jnp.where(lane_at < width, noise * own_d, 0.0)
    ag_send[...] = jnp.where(lane_at < mid_lane, a_own, norm_red)
    to_con(3, ag_send, ag_con)
    to_red(4, ag_send, ag_red)
    ag_con[me_con] = ag_send[...]
    ag_red[me_red] = ag_send[...]

    arrive(recv_sem.at[3], ag_con, n_con)
    total = jnp.sum(ag_con[...], axis=0)
    res_norm = total[:, mid_lane : mid_lane + 1]
    curvature = total[:, width : width + 1] + noise * res_norm
    step_size = res_norm / curvature
    for t in range(NZ):
        for c in range(CORES):
            at = t * pair + c * width
            con_a[:, at : at + width] = ag_con[near[t] * CORES + c, :, 0:width]
    r_con = d_con - step_size * con_a[...]
    nrm_send[...] = to_row(jnp.sum(r_con * r_con, axis=1, keepdims=True), 0)
    to_red(5, nrm_send, nrm_recv)
    nrm_recv[me_red] = nrm_send[...]
    arrive(recv_sem.at[4], ag_red, n_red)
    for k in range(n_red):
        red_a[:, k * width : (k + 1) * width] = ag_red[k, :, 0:width]
    r_red = d_red - step_size * red_a[...]
    r_own = own_d - step_size * a_own
    arrive(recv_sem.at[5], nrm_recv, n_red)
    fresh_norm = to_column(jnp.sum(nrm_recv[...], axis=0), 0)
    beta = fresh_norm / res_norm
    d1_con = r_con + beta * d_con
    for p in range(n_part):
        blocks[:, p * span : (p + 1) * span] = jnp.where(mine[p], d1_con, 0.0).astype(BF16)
    d1_red = r_red + beta * d_red
    d1_own = r_own + beta * own_d

    done = 0
    for jb in range(wide // TILE):
        cols = slice(jb * TILE, (jb + 1) * TILE)
        product[:, cols] = jnp.dot(blocks[...], kept[:, cols], preferred_element_type=F32)
        while (done + 1) * width <= (jb + 1) * TILE:
            chunk_out(done, rs2_send, jnp.zeros((count, 1), F32))
            done += 1
    crv_send[...] = to_row(jnp.sum(d1_red * product[...], axis=1, keepdims=True), 0)
    to_red(8, crv_send, crv_recv)
    for at, peer in red_peers:
        send(6, peer, rs2_send.at[at], rs2_recv.at[me_red])
    crv_recv[me_red] = crv_send[...]
    norm1 = to_row(jnp.sum(d1_red * d1_red, axis=1, keepdims=True), count)
    arrive(recv_sem.at[8], crv_recv, n_red)
    fin_send[...] = jnp.sum(crv_recv[...], axis=0) + norm1
    to_con(7, fin_send, fin_recv)
    fin_recv[me_con] = fin_send[...]
    rs2_recv[me_red] = rs2_send[me_red]
    arrive(recv_sem.at[6], rs2_recv, n_red)
    a1_own = jnp.sum(rs2_recv[...], axis=0) + noise * d1_own
    drain((0, 1, 2, 3, 4, 5, 6, 8, 9))
    arrive(recv_sem.at[7], fin_recv, n_con)
    total = jnp.sum(fin_recv[...], axis=0)
    step1 = fresh_norm / (to_column(total, 0) + noise * to_column(total, count))
    sol = step_size * own_d + step1 * d1_own
    res = r_own - step1 * a1_own
    sol_out[...] = sol[:, 0:width]
    res_out[...] = res[:, 0:width]
    drain((7,))


def solution(mesh):
    n_red, n_con = NX * NY, NZ * CORES

    def on_device(points, targets, probes, lengthscale, outputscale, noise_var):
        feats, width = points.shape
        n_part = lengthscale.shape[0]
        per = probes.shape[0] // n_part + 1
        count = n_part * per
        pair, span, wide = CORES * width, n_con * width, n_red * width
        whole = pl.cdiv(feats * width // 8 + 2 * width, LANES) * LANES
        base = feats * width // 8
        vmem = pl.BlockSpec(memory_space=pltpu.VMEM)
        anywhere = pl.BlockSpec(memory_space=pl.ANY)
        out = jax.ShapeDtypeStruct((count, width), F32)

        def slots(n, *shape):
            return pltpu.VMEM((n, *(shape or (count, LANES))), F32)

        row = pltpu.VMEM((1, LANES), F32)
        return pl.pallas_call(
            functools.partial(kernel, width, per),
            out_shape=(out, out),
            in_specs=[anywhere] * 6,
            out_specs=(vmem, vmem),
            scratch_shapes=[
                pltpu.VMEM((feats, width), F32),
                pltpu.VMEM((1, width), F32),
                pltpu.VMEM(probes.shape, F32),
                pltpu.SMEM((n_part,), F32),
                pltpu.SMEM((n_part,), F32),
                pltpu.SMEM((n_part,), F32),
                pltpu.VMEM((count, LANES), F32),
                pltpu.VMEM((8, whole), F32),
                slots(n_con, 8, whole),
                slots(n_red, 8, base),
                slots(n_red, 8, whole - base),
                pltpu.VMEM((2, pair, TILE), BF16),
                pltpu.VMEM((NZ, count, TILE), F32),
                pltpu.VMEM((feats, wide), F32),
                pltpu.VMEM((TILE, wide), BF16),
                pltpu.VMEM((count, span), F32),
                pltpu.VMEM((count, wide), F32),
                pltpu.VMEM((count, span), F32),
                pltpu.VMEM((count, wide), F32),
                pltpu.VMEM((count, n_part * span), BF16),
                pltpu.VMEM((wide // TILE, pair, TILE), F32),
                pltpu.VMEM((n_part * span, wide), BF16),
                pltpu.VMEM((count, wide), F32),
                slots(n_red),
                slots(n_red),
                pltpu.VMEM((count, LANES), F32),
                slots(n_con),
                slots(n_red),
                row,
                slots(n_red, 1, LANES),
                slots(n_red),
                slots(n_red),
                row,
                slots(n_red, 1, LANES),
                row,
                slots(n_con, 1, LANES),
                pltpu.SemaphoreType.DMA((6,)),
                pltpu.SemaphoreType.DMA((10,)),
                pltpu.SemaphoreType.DMA((10,)),
                pltpu.SemaphoreType.DMA((n_con,)),
            ],
            compiler_params=pltpu.CompilerParams(
                collective_id=0, has_side_effects=True, vmem_limit_bytes=56 * 2**20
            ),
            name="cg_solve",
        )(points, targets[None, :], probes, lengthscale, outputscale, noise_var)

    both = P(None, ("row", "col"))
    return jax.shard_map(
        on_device,
        mesh=mesh,
        in_specs=(both, P(("row", "col")), both, P(), P(), P()),
        out_specs=(both, both),
        check_vma=False,
    )
```

time: 73.1 us -> 57.7 us (0.79)
  Pallas kernels: 70.1 us -> 55 us
    pallas_call x1, Pallas kernels: 70.1 us -> 55 us  [on_device(): pl.pallas_call(functools.partial(kernel, width, per), out_shape=(out, out...]
where the time goes in v2:
time: 57.7 us; the launch traced here: 57.5 us
  Pallas kernels  55 us (95%)
  local copies, waits for them, and re-layouts  1.9 us (3%)
  between operations  0.65 us (1%)
    pallas_call x1, Pallas kernels, on_device(): pl.pallas_call(functools.partial(kernel, width, per), out_shape=(out, out...  55 us
    unnamed x4, local copies, waits for them, and re-layouts  1.9 us

profile of v2, /device:TPU:1, one launch (start us, length us, event | category | flops | bytes accessed | tf_op | source)
XLA Modules:
  0.0 57.5 jit_solution(1684135333780530887)
XLA Ops:
  0.6 55.0 %cg_solve.1 = (f32[12,96]{1,0:T(8,128)}, f32[12,96]{1,0:T(8,128)}) custom-call(f32[32,96]{1,0:T(8,128)} %points_hbm.1, f32[1,96]{1,0:T(1,128)} %bitcast.1, f32[8,96]{1,0:T(8,128)} %probes_hbm.1, f32[4]{0:T(128)} %lengthscale_hbm.1, f32[4]{0:T(128)} %outputscale_hbm.1, f32[4]{0:T(128)} %noise_hbm.1), custom_call_target="tpu_custom_call" | custom-call | tf_op jit(solution)/shard_map/cg_solve/pallas_call | solution.py:386
  55.6 0.0 copy-start
  55.6 1.3 %copy.10 = f32[12,96]{1,0:T(8,128)} copy(f32[12,96]{1,0:T(8,128)} %get-tuple-element.4) | data formatting | bytes 9216
  56.9 0.0 copy-done
  56.9 0.6 %copy.11 = f32[12,96]{1,0:T(8,128)} copy(f32[12,96]{1,0:T(8,128)S(1)} %copy-done) | data formatting | bytes 9216
Async XLA Ops:
  55.6 1.3 %copy-start = (f32[12,96]{1,0:T(8,128)S(1)}, f32[12,96]{1,0:T(8,128)}, u32[]{:S(2)}) copy-start(f32[12,96]{1,0:T(8,128)} %get-tuple-element.5) | copy-start | bytes 13828

commit v3 on v2

--- a/solution.py
+++ b/solution.py
@@ -57,7 +57,8 @@
     con_in,
     red_in,
     red_rhs_in,
-    con_lhs,
+    lhs_even,
+    lhs_odd,
     con_dt,
     red_x,
     red_op,
@@ -66,16 +67,20 @@
     con_a,
     red_a,
     blocks,
-    dist,
-    kept,
+    dist_even,
+    dist_odd,
+    kept_even,
+    kept_odd,
     product,
     rs_send,
     rs_recv,
     ag_send,
     ag_con,
     ag_red,
-    nrm_send,
-    nrm_recv,
+    mom_send,
+    mom_recv,
+    sum_send,
+    sum_recv,
     rs2_send,
     rs2_recv,
     crv_send,
@@ -141,7 +146,7 @@
         pltpu.make_async_copy(some, some, sem).wait()
 
     def drain(phases):
-        buffers = (con_in, red_in, rs_recv, ag_con, ag_red, nrm_recv, rs2_recv, fin_recv, crv_recv, red_rhs_in)
+        buffers = (con_in, red_in, rs_recv, ag_con, ag_red, mom_recv, rs2_recv, fin_recv, crv_recv, red_rhs_in, sum_recv)
         for phase in phases:
             arrive(send_sem.at[phase], buffers[phase], buffers[phase].shape[0])
 
@@ -172,6 +177,11 @@
         length = jnp.full((1, TILE), lengthscale[p], F32)
         scales.append(((-0.5 * LOG2E) / (length * length), jnp.full((1, TILE), outputscale[p], F32)))
     product[...] = jnp.zeros_like(product)
+    half = span // 2
+    con_dt[NZ] = jnp.zeros_like(con_dt[NZ])
+    for p in range(n_part):
+        last = p * half + half - pair
+        kept_odd[last : last + pair, :] = jnp.zeros((pair, wide), BF16)
 
     pl.semaphore_wait(barrier, n_red - 1 + n_con - 1)
 
@@ -193,10 +203,8 @@
         for _, peer in red_peers:
             send(phase, peer, src, slots.at[me_red])
 
-    for _, peer in con_peers[:5]:
-        send(0, peer, msg, con_in.at[me_con], con_sem.at[me_con])
     to_red(1, msg.at[:, 0:base], red_in)
-    for _, peer in con_peers[5:]:
+    for _, peer in con_peers:
         send(0, peer, msg, con_in.at[me_con], con_sem.at[me_con])
     to_red(9, msg.at[:, base:], red_rhs_in)
     con_in[me_con] = msg[...]
@@ -208,7 +216,7 @@
     def con_wait(slot):
         pltpu.make_async_copy(con_in.at[slot], con_in.at[slot], con_sem.at[slot]).wait()
 
-    def prepare(t, z, buf):
+    def prepare(t, z, lhs):
         for c in range(CORES):
             slot = z * CORES + c
             x = jnp.concatenate(
@@ -217,35 +225,39 @@
             hi, mid, low = split3(x)
             norms = norm_rows(split3(jnp.sum(x * x, axis=0, keepdims=True)), False)
             full = jnp.concatenate([hi, hi, mid, hi, mid, low, norms, pad], axis=0)
-            con_lhs[buf, c * width : (c + 1) * width, :] = jnp.transpose(full)[0:width].astype(BF16)
+            lhs[c * width : (c + 1) * width, :] = jnp.transpose(full)[0:width].astype(BF16)
             con_dt[t, 0:8, c * width : (c + 1) * width] = con_in[slot, :, base : base + width]
             con_dt[t, 8:count, c * width : (c + 1) * width] = con_in[
                 slot, 0 : count - 8, base + width : base + 2 * width
             ]
 
-    def build(t, buf):
-        low = con_dt[t, :, 0:pair]
-        sides = [jnp.where(mine[p], low, 0.0).astype(BF16) for p in range(n_part)]
-        lhs = con_lhs[buf]
-        for jb in range(wide // TILE):
-            cols = slice(jb * TILE, (jb + 1) * TILE)
-            dist[jb] = jnp.dot(lhs, red_op[:, cols], preferred_element_type=F32)
-        for jb in range(wide // TILE):
-            cols = slice(jb * TILE, (jb + 1) * TILE)
+    tiles = [slice(jb * TILE, (jb + 1) * TILE) for jb in range(wide // TILE)]
+
+    def distances(lhs, dist):
+        for jb, cols in enumerate(tiles):
+            dist[jb] = jnp.dot(lhs[...], red_op[:, cols], preferred_element_type=F32)
+
+    def exponentials(i, dist, kept):
+        for jb, cols in enumerate(tiles):
             for r in range(pair // CHUNK):
                 part = dist[jb, r * CHUNK : (r + 1) * CHUNK, :]
                 for p in range(n_part):
                     kern = (scales[p][1] * jnp.exp2(part * scales[p][0])).astype(BF16)
-                    at = pl.multiple_of(p * span + t * pair + r * CHUNK, CHUNK)
+                    at = pl.multiple_of(i * pair, CHUNK) + p * half + r * CHUNK
                     kept[pl.ds(at, CHUNK), cols] = kern
+
+    def multiply(t, i, kept):
+        low = con_dt[t, :, 0:pair]
+        sides = [jnp.where(mine[p], low, 0.0).astype(BF16) for p in range(n_part)]
+        for cols in tiles:
             total = product[:, cols]
             for p in range(n_part):
-                at = pl.multiple_of(p * span + t * pair, CHUNK)
+                at = pl.multiple_of(i * pair, CHUNK) + p * half
                 total = total + jnp.dot(sides[p], kept[pl.ds(at, pair), cols], preferred_element_type=F32)
             product[:, cols] = total
 
     con_wait(at_z * CORES + 1 - core)
-    prepare(0, at_z, 0)
+    prepare(0, at_z, lhs_even)
 
     arrive(recv_sem.at[1], red_in, n_red)
     for k in range(n_red):
@@ -258,25 +270,42 @@
     pad2 = jnp.zeros((TILE - 6 * feats - 16, wide), F32)
     red_op[...] = jnp.concatenate([hi, mid, hi, low, mid, hi, norms, pad2], axis=0).astype(BF16)
 
-    def step(t, _):
-        z = near_z(t + 1)
+    distances(lhs_even, dist_even)
+
+    last = NZ // 2 - 1
+
+    def steps(i, _):
+        z = near_z(2 * i + 1)
         con_wait(z * CORES)
         con_wait(z * CORES + 1)
-        build(t, lax.rem(t, 2))
-        prepare(t + 1, z, lax.rem(t + 1, 2))
+        multiply(lax.rem(2 * i + NZ, NZ + 1), lax.rem(i + last, NZ // 2), kept_odd)
+        prepare(2 * i + 1, z, lhs_odd)
+        distances(lhs_odd, dist_odd)
+        exponentials(i, dist_even, kept_even)
+        z = near_z(2 * i + 2)
+
+        @pl.when(i < last)
+        def _():
+            con_wait(z * CORES)
+            con_wait(z * CORES + 1)
+
+        multiply(2 * i, i, kept_even)
+        prepare(2 * i + 2, z, lhs_even)
+        distances(lhs_even, dist_even)
+        exponentials(i, dist_odd, kept_odd)
         return 0
 
-    lax.fori_loop(0, NZ - 1, step, 0)
-    build(NZ - 1, (NZ - 1) % 2)
+    lax.fori_loop(0, NZ // 2, steps, 0)
+    multiply(NZ - 1, last, kept_odd)
 
     arrive(recv_sem.at[9], red_rhs_in, n_red)
     for k in range(n_red):
         red_d[0:8, k * width : (k + 1) * width] = red_rhs_in[k, :, 0:width]
         red_d[8:count, k * width : (k + 1) * width] = red_rhs_in[k, 0 : count - 8, width : 2 * width]
 
-    def chunk_out(k, buf, extra):
+    def chunk_out(k, buf):
         buf[k, :, 0:width] = product[:, k * width : (k + 1) * width]
-        buf[k, :, width:LANES] = jnp.broadcast_to(extra, (count, LANES - width))
+        buf[k, :, width:LANES] = jnp.zeros((count, LANES - width), F32)
 
     def to_row(column, offset):
         return jnp.sum(jnp.where(lane_at == row_at + offset, column, 0.0), axis=0, keepdims=True)
@@ -284,61 +313,102 @@
     def to_column(row, offset):
         return jnp.sum(jnp.where(lane_at == row_at + offset, row, 0.0), axis=1, keepdims=True)
 
-    mid_lane = (width + LANES) // 2
     own_d = rhs[...]
     d_red = red_d[...]
-    partial_curve = jnp.sum(d_red * product[...], axis=1, keepdims=True)
     for k in range(n_red):
-        chunk_out(k, rs_send, partial_curve)
+        chunk_out(k, rs_send)
     for at, peer in red_peers:
         send(2, peer, rs_send.at[at], rs_recv.at[me_red])
     rs_recv[me_red] = rs_send[me_red]
     for t in range(NZ):
         con_d[:, t * pair : (t + 1) * pair] = con_dt[t, :, 0:pair]
     d_con = con_d[...]
-    norm_red = jnp.sum(d_red * d_red, axis=1, keepdims=True)
     arrive(recv_sem.at[2], rs_recv, n_red)
-    a_own = jnp.sum(rs_recv[...], axis=0)
-    a_own = a_own + jnp.where(lane_at < width, noise * own_d, 0.0)
-    ag_send[...] = jnp.where(lane_at < mid_lane, a_own, norm_red)
+    a_own = jnp.sum(rs_recv[...], axis=0) + noise * own_d
+    ag_send[...] = a_own
+
+    def over_lanes(v):
+        return jnp.sum(jnp.where(lane_at < width, v, 0.0), axis=1, keepdims=True)
+
+    dd, da, aa = over_lanes(own_d * own_d), over_lanes(own_d * a_own), over_lanes(a_own * a_own)
+    guess = jnp.where(da * 16.0 > dd, dd / jnp.where(da > 0.0, da, 1.0), 0.0)
+    left = own_d - guess * a_own
+    mom_send[...] = (
+        to_row(guess, 0)
+        + to_row(over_lanes(left * left), count)
+        + to_row(over_lanes(left * a_own), 2 * count)
+        + to_row(aa, 3 * count)
+        + to_row(dd, 4 * count)
+        + to_row(da, 5 * count)
+    )
+    to_red(5, mom_send, mom_recv)
     to_con(3, ag_send, ag_con)
     to_red(4, ag_send, ag_red)
+    mom_recv[me_red] = mom_send[...]
     ag_con[me_con] = ag_send[...]
     ag_red[me_red] = ag_send[...]
 
+    def merge(slots):
+        rows = jnp.concatenate([slots[k] for k in range(slots.shape[0])], axis=0)
+
+        def field(f):
+            return rows if f == 0 else pltpu.roll(rows, LANES - f * count, 1)
+
+        def add(v):
+            return jnp.sum(v, axis=0, keepdims=True)
+
+        dd, da = add(field(4)), add(field(5))
+        ok = da * 16.0 > dd
+        guess = jnp.where(ok, dd / jnp.where(ok, da, 1.0), 0.0)
+        off = field(0) - guess
+        a_sq, cross, base_sq = field(3), field(2), field(1)
+        cross_new = cross + off * a_sq
+        base_new = base_sq + off * (cross + cross_new)
+        return guess, add(base_new), add(cross_new), add(a_sq), dd, da
+
+    arrive(recv_sem.at[5], mom_recv, n_red)
+    packed = jnp.zeros((1, LANES), F32)
+    lane_row = lax.broadcasted_iota(jnp.int32, (1, LANES), 1)
+    for f, value in enumerate(merge(mom_recv)):
+        moved = value if f == 0 else pltpu.roll(value, f * count, 1)
+        packed = jnp.where((lane_row >= f * count) & (lane_row < (f + 1) * count), moved, packed)
+    sum_send[...] = packed
+    to_con(10, sum_send, sum_recv)
+    sum_recv[me_con] = sum_send[...]
+
     arrive(recv_sem.at[3], ag_con, n_con)
-    total = jnp.sum(ag_con[...], axis=0)
-    res_norm = total[:, mid_lane : mid_lane + 1]
-    curvature = total[:, width : width + 1] + noise * res_norm
-    step_size = res_norm / curvature
     for t in range(NZ):
         for c in range(CORES):
             at = t * pair + c * width
             con_a[:, at : at + width] = ag_con[near[t] * CORES + c, :, 0:width]
-    r_con = d_con - step_size * con_a[...]
-    nrm_send[...] = to_row(jnp.sum(r_con * r_con, axis=1, keepdims=True), 0)
-    to_red(5, nrm_send, nrm_recv)
-    nrm_recv[me_red] = nrm_send[...]
     arrive(recv_sem.at[4], ag_red, n_red)
     for k in range(n_red):
         red_a[:, k * width : (k + 1) * width] = ag_red[k, :, 0:width]
+    arrive(recv_sem.at[10], sum_recv, n_con)
+    step_row, fresh_row, _, _, norm_row, _ = merge(sum_recv)
+    step_size = to_column(step_row, 0)
+    fresh_norm, res_norm = to_column(fresh_row, 0), to_column(norm_row, 0)
+    r_con = d_con - step_size * con_a[...]
     r_red = d_red - step_size * red_a[...]
     r_own = own_d - step_size * a_own
-    arrive(recv_sem.at[5], nrm_recv, n_red)
-    fresh_norm = to_column(jnp.sum(nrm_recv[...], axis=0), 0)
     beta = fresh_norm / res_norm
     d1_con = r_con + beta * d_con
     for p in range(n_part):
-        blocks[:, p * span : (p + 1) * span] = jnp.where(mine[p], d1_con, 0.0).astype(BF16)
+        low = jnp.where(mine[p], d1_con, 0.0).astype(BF16)
+        for t in range(NZ):
+            at = (t % 2) * n_part * half + p * half + (t // 2) * pair
+            blocks[:, at : at + pair] = low[:, t * pair : (t + 1) * pair]
     d1_red = r_red + beta * d_red
     d1_own = r_own + beta * own_d
 
     done = 0
     for jb in range(wide // TILE):
         cols = slice(jb * TILE, (jb + 1) * TILE)
-        product[:, cols] = jnp.dot(blocks[...], kept[:, cols], preferred_element_type=F32)
+        product[:, cols] = jnp.dot(
+            blocks[:, 0 : n_part * half], kept_even[:, cols], preferred_element_type=F32
+        ) + jnp.dot(blocks[:, n_part * half :], kept_odd[:, cols], preferred_element_type=F32)
         while (done + 1) * width <= (jb + 1) * TILE:
-            chunk_out(done, rs2_send, jnp.zeros((count, 1), F32))
+            chunk_out(done, rs2_send)
             done += 1
     crv_send[...] = to_row(jnp.sum(d1_red * product[...], axis=1, keepdims=True), 0)
     to_red(8, crv_send, crv_recv)
@@ -353,7 +423,7 @@
     rs2_recv[me_red] = rs2_send[me_red]
     arrive(recv_sem.at[6], rs2_recv, n_red)
     a1_own = jnp.sum(rs2_recv[...], axis=0) + noise * d1_own
-    drain((0, 1, 2, 3, 4, 5, 6, 8, 9))
+    drain((0, 1, 2, 3, 4, 5, 6, 8, 9, 10))
     arrive(recv_sem.at[7], fin_recv, n_con)
     total = jnp.sum(fin_recv[...], axis=0)
     step1 = fresh_norm / (to_column(total, 0) + noise * to_column(total, count))
@@ -400,8 +470,9 @@
                 slots(n_con, 8, whole),
                 slots(n_red, 8, base),
                 slots(n_red, 8, whole - base),
-                pltpu.VMEM((2, pair, TILE), BF16),
-                pltpu.VMEM((NZ, count, TILE), F32),
+                pltpu.VMEM((pair, TILE), BF16),
+                pltpu.VMEM((pair, TILE), BF16),
+                pltpu.VMEM((NZ + 1, count, TILE), F32),
                 pltpu.VMEM((feats, wide), F32),
                 pltpu.VMEM((TILE, wide), BF16),
                 pltpu.VMEM((count, span), F32),
@@ -410,7 +481,9 @@
                 pltpu.VMEM((count, wide), F32),
                 pltpu.VMEM((count, n_part * span), BF16),
                 pltpu.VMEM((wide // TILE, pair, TILE), F32),
-                pltpu.VMEM((n_part * span, wide), BF16),
+                pltpu.VMEM((wide // TILE, pair, TILE), F32),
+                pltpu.VMEM((n_part * span // 2, wide), BF16),
+                pltpu.VMEM((n_part * span // 2, wide), BF16),
                 pltpu.VMEM((count, wide), F32),
                 slots(n_red),
                 slots(n_red),
@@ -419,6 +492,8 @@
                 slots(n_red),
                 row,
                 slots(n_red, 1, LANES),
+                row,
+                slots(n_con, 1, LANES),
                 slots(n_red),
                 slots(n_red),
                 row,
@@ -426,8 +501,8 @@
                 row,
                 slots(n_con, 1, LANES),
                 pltpu.SemaphoreType.DMA((6,)),
-                pltpu.SemaphoreType.DMA((10,)),
-                pltpu.SemaphoreType.DMA((10,)),
+                pltpu.SemaphoreType.DMA((11,)),
+                pltpu.SemaphoreType.DMA((11,)),
                 pltpu.SemaphoreType.DMA((n_con,)),
             ],
             compiler_params=pltpu.CompilerParams(

time: 57.7 us -> 55 us (0.953)
  Pallas kernels: 55 us -> 52.2 us
    pallas_call x1, Pallas kernels: 55 us -> 52.2 us  [on_device(): pl.pallas_call(functools.partial(kernel, width, per), out_shape=(out, out...]
where the time goes in v3:
time: 55 us; the launch traced here: 54.8 us
  Pallas kernels  52.2 us (95%)
  local copies, waits for them, and re-layouts  1.9 us (3%)
  between operations  0.65 us (1%)
    pallas_call x1, Pallas kernels, on_device(): pl.pallas_call(functools.partial(kernel, width, per), out_shape=(out, out...  52.2 us
    unnamed x4, local copies, waits for them, and re-layouts  1.9 us

profile of v3, /device:TPU:1, one launch (start us, length us, event | category | flops | bytes accessed | tf_op | source)
XLA Modules:
  0.0 54.8 jit_solution(13604351566575741177)
XLA Ops:
  0.6 52.2 %cg_solve.1 = (f32[12,96]{1,0:T(8,128)}, f32[12,96]{1,0:T(8,128)}) custom-call(f32[32,96]{1,0:T(8,128)} %points_hbm.1, f32[1,96]{1,0:T(1,128)} %bitcast.1, f32[8,96]{1,0:T(8,128)} %probes_hbm.1, f32[4]{0:T(128)} %lengthscale_hbm.1, f32[4]{0:T(128)} %outputscale_hbm.1, f32[4]{0:T(128)} %noise_hbm.1), custom_call_target="tpu_custom_call" | custom-call | tf_op jit(solution)/shard_map/cg_solve/pallas_call | solution.py:456
  52.9 0.0 copy-start
  52.9 1.3 %copy.10 = f32[12,96]{1,0:T(8,128)} copy(f32[12,96]{1,0:T(8,128)} %get-tuple-element.4) | data formatting | bytes 9216
  54.2 0.0 copy-done
  54.2 0.6 %copy.11 = f32[12,96]{1,0:T(8,128)} copy(f32[12,96]{1,0:T(8,128)S(1)} %copy-done) | data formatting | bytes 9216
Async XLA Ops:
  52.9 1.3 %copy-start = (f32[12,96]{1,0:T(8,128)S(1)}, f32[12,96]{1,0:T(8,128)}, u32[]{:S(2)}) copy-start(f32[12,96]{1,0:T(8,128)} %get-tuple-element.5) | copy-start | bytes 13828
